TPU v7x, 32 devices: a whole 2x2x4 slice. The times are simulated.
32 devices in a mesh: gx: 4 (over x, core), gy: 4 (over z), gz: 2 (over y).
Axes of the slice: x: 2, y: 2, z: 4, core: 2. Of those that a mesh axis runs over, the one named last changes fastest.
Arguments:
- fine_coef: bfloat16 [256, 512], P(('gx', 'gy', 'gz')), may hold values from -6 to 6
- mid_leaf: bfloat16 [32, 512], P(('gx', 'gy', 'gz')), may hold values from -6 to 6
- mid_child: int32 [32, 8], P(('gx', 'gy', 'gz')), may hold values from 0 to 7, as said below
- mid_parent: int32 [32], P(('gx', 'gy', 'gz')), may hold values from 0 to 31, each once
- mid_refined: int32 [32], P(('gx', 'gy', 'gz')), may hold values 0 or 1
- fine_nbr: int32 [256, 27], P(('gx', 'gy', 'gz')), may hold values from -1 to 255, as said below
- mid_nbr: int32 [32, 27], P(('gx', 'gy', 'gz')), may hold values from -1 to 31, as said below
- coarse_nbr: int32 [4, 27], replicated, may hold values from -1 to 3, as said below
- op_factor: float32 [3, 32, 3, 8, 8], replicated, may hold values from -1 to 1
- term_weight: float32 [32], replicated, may hold values from 0.05 to 1
Outputs:
- fine_out: float32 [256, 512], P(('gx', 'gy', 'gz'))
- mid_out: float32 [32, 512], P(('gx', 'gy', 'gz'))
Inputs may be any that keep to these rules, and one draw needn't show every extreme that they name: `fine_nbr`: column d names the fine box adjacent across displacement (d // 9 - 1, d // 3 % 3 - 1, d % 3 - 1), or -1. Column 13 is the row's own box. Box g lies on device g // 8; the named box's device differs from the row's device along each of gx, gy, gz by 0 or by that component of the displacement. `mid_nbr`: column d names the middle box adjacent across displacement (d // 9 - 1, d // 3 % 3 - 1, d % 3 - 1), or -1. Column 13 is the row's own box. Box g lies on device g; the named box's device differs from the row's device along each of gx, gy, gz by 0 or by that component of the displacement. `coarse_nbr`: column d names the coarse box adjacent across displacement (d // 9 - 1, d // 3 % 3 - 1, d % 3 - 1), or -1. Column 13 is the row's own box. `mid_child`: the 1 row of one device together name each of its 8 local fine slots exactly once. `mid_parent`: each value appears once.
All inputs are finite; a program needn't handle non-finite values. No bound on the sum of `mid_refined` on one device may be relied on, other than what follows from the above.
Results may differ from a plain program's by a relative error of at most 0.006.
Values may be sent and summed in bfloat16 or wider, within the bound.
A program may use at most 64 MiB of HBM per device.

v0:
```python
import math
import jax
import jax.numpy as jnp
import numpy as np
from jax import lax
from jax.sharding import PartitionSpec as P

exact_mode = lax.Precision.HIGHEST


def padded_2(cells, sides, width):
    for axis, dim in sides:
        count = lax.axis_size(axis)
        ends = count - 1
        head = lax.slice_in_dim(cells, 0, width, axis=dim)
        tail = lax.slice_in_dim(cells, cells.shape[dim] - width, cells.shape[dim], axis=dim)
        cells = jnp.concatenate(
            [
                lax.ppermute(tail, axis, [(i, (i + 1) % count) for i in range(ends)]),
                cells,
                lax.ppermute(head, axis, [((i + 1) % count, i) for i in range(ends)]),
            ],
            axis=dim,
        )
    return cells


def poly_multiply(left, right):
    result = [0.0] * (len(left) + len(right) - 1)
    for first, left_coef in enumerate(left):
        for second, right_coef in enumerate(right):
            result[first + second] += left_coef * right_coef
    return result


def poly_compose(coeffs, factor, offset):
    result = [0.0]
    power_term = [1.0]
    for coef in coeffs:
        padded = result + [0.0] * (len(power_term) - len(result))
        result = [padded[place] + coef * power_term[place] for place in range(len(power_term))]
        power_term = poly_multiply(power_term, [offset, factor])
    return result


def legendre_table(basis_order):
    polys = [[1.0], [0.0, 1.0]]
    for degree in range(1, basis_order):
        upper = [0.0] + [(2 * degree + 1) * coef for coef in polys[degree]]
        lower = [degree * coef for coef in polys[degree - 1]] + [0.0] * (
            len(upper) - len(polys[degree - 1])
        )
        polys.append([(upper[place] - lower[place]) / (degree + 1) for place in range(len(upper))])
    return [
        [math.sqrt(2 * degree + 1) * coef for coef in poly_compose(polys[degree], 2.0, -1.0)]
        for degree in range(basis_order)
    ]


def two_scale(basis_order):
    shifted = legendre_table(basis_order)
    filters = np.zeros((2, basis_order, basis_order))
    for which_half in range(2):
        for row_at in range(basis_order):
            halved = poly_compose(shifted[row_at], 0.5, 0.5 * which_half)
            for col_at in range(basis_order):
                product = poly_multiply(halved, shifted[col_at])
                total = sum((coef / (place + 1) for place, coef in enumerate(product)))
                filters[which_half, row_at, col_at] = total / math.sqrt(2.0)
    return jnp.asarray(filters, jnp.float32)


def compress(children, filters):
    box_count = children.shape[0]
    basis_order = filters.shape[1]
    cube_form = children.reshape(box_count, 2, 2, 2, basis_order, basis_order, basis_order)
    section_one = jnp.einsum("bijlxyz,ipx->bjlpyz", cube_form, filters, precision=exact_mode)
    section_two = jnp.einsum("bjlpyz,jqy->blpqz", section_one, filters, precision=exact_mode)
    section_three = jnp.einsum("blpqz,lrz->bpqr", section_two, filters, precision=exact_mode)
    return section_three.reshape(box_count, basis_order**3)


def prolong(parents, filters):
    box_count = parents.shape[0]
    basis_order = filters.shape[1]
    cube_form = parents.reshape(box_count, basis_order, basis_order, basis_order)
    section_one = jnp.einsum("bpqr,ipx->bixqr", cube_form, filters, precision=exact_mode)
    section_two = jnp.einsum("bixqr,jqy->bijxyr", section_one, filters, precision=exact_mode)
    section_three = jnp.einsum("bijxyr,lrz->bijlxyz", section_two, filters, precision=exact_mode)
    return section_three.reshape(box_count, 8, basis_order**3)


def level_tables(factors, weights):
    basis_order = factors.shape[-1]
    term_count = factors.shape[0]
    plane_size = basis_order * basis_order
    row_total = term_count * plane_size
    row_id = jnp.arange(row_total, dtype=jnp.int32)
    term_of = row_id // plane_size
    first_of = row_id // basis_order % basis_order
    second_of = row_id % basis_order
    pair_id = jnp.arange(term_count * basis_order, dtype=jnp.int32)
    select_first = ((term_of * basis_order + first_of)[:, None] == pair_id[None, :]).astype(
        jnp.float32
    )
    select_second = ((term_of * basis_order + second_of)[:, None] == pair_id[None, :]).astype(
        jnp.float32
    )
    col_id = jnp.arange(plane_size, dtype=jnp.int32)
    order_id = jnp.arange(basis_order, dtype=jnp.int32)
    spread_outer = (order_id[:, None] == (col_id // basis_order)[None, :]).astype(jnp.float32)
    spread_inner = (order_id[:, None] == (col_id % basis_order)[None, :]).astype(jnp.float32)
    across = jnp.transpose(factors, (1, 0, 3, 2)).reshape(3, term_count * basis_order, basis_order)
    left_pick = jnp.einsum("rs,esb->erb", select_first, across, precision=exact_mode)
    left_full = jnp.einsum("erb,bq->erq", left_pick, spread_outer, precision=exact_mode)
    right_pick = jnp.einsum("rs,esc->erc", select_second, across, precision=exact_mode)
    right_full = jnp.einsum("erc,cq->erq", right_pick, spread_inner, precision=exact_mode)
    weight_rows = jnp.dot(select_first, jnp.repeat(weights, basis_order), precision=exact_mode)
    blocks = weight_rows[None, None, :, None] * left_full[:, None] * right_full[None, :]
    return (factors.astype(jnp.bfloat16), blocks.astype(jnp.bfloat16))


def apply_boxes(sources, factor_bf, blocks):
    box_count = sources.shape[0]
    basis_order = factor_bf.shape[-1]
    plane_size = basis_order * basis_order
    cube_form = sources.reshape(box_count, 3, 3, 3, basis_order, plane_size)
    running = jnp.zeros((box_count * basis_order, plane_size), jnp.float32)
    for along_y in range(3):
        for along_z in range(3):
            picked = cube_form[:, :, along_y, along_z]
            mixed_terms = jnp.einsum(
                "mdax,bdxq->bamq", factor_bf, picked, preferred_element_type=jnp.float32
            ).astype(jnp.bfloat16)
            flat_terms = mixed_terms.reshape(box_count * basis_order, -1)
            running = running + jnp.dot(
                flat_terms, blocks[along_y, along_z], preferred_element_type=jnp.float32
            )
    return running.reshape(box_count, basis_order**3)


def pick_sources(source_table, near_ids):
    return source_table[jnp.maximum(near_ids, 0)] * (near_ids >= 0)[:, :, None].astype(jnp.bfloat16)


def apply_picked(source_table, near_ids, factor_bf, blocks):
    total_rows = near_ids.shape[0]
    group_rows = math.gcd(total_rows, 16)
    grouped = near_ids.reshape(total_rows // group_rows, group_rows, 27)

    def one_group(some_rows):
        return apply_boxes(pick_sources(source_table, some_rows), factor_bf, blocks)

    return lax.map(one_group, grouped).reshape(total_rows, -1)


def local_rows(near_ids, per_device):
    size_y = lax.axis_size("gy")
    size_z = lax.axis_size("gz")
    mine_x = lax.axis_index("gx")
    mine_y = lax.axis_index("gy")
    mine_z = lax.axis_index("gz")
    device = near_ids // per_device
    slot_at = near_ids % per_device
    other_x = device // (size_y * size_z)
    other_y = device // size_z % size_y
    other_z = device % size_z
    cell_at = (other_x - mine_x + 1) * 9 + (other_y - mine_y + 1) * 3 + (other_z - mine_z + 1)
    return jnp.where(near_ids >= 0, cell_at * per_device + slot_at, -1)


def near_fine(detail):
    shaped = detail.reshape((1, 1, 1) + detail.shape)
    extended = padded_2(shaped, (("gx", 0), ("gy", 1), ("gz", 2)), 1)
    return extended.reshape(-1, detail.shape[1])


def near_mid(detail):
    shaped = detail.reshape((1, 1, 1) + detail.shape)
    extended = padded_2(shaped, (("gx", 0), ("gy", 1), ("gz", 2)), 1)
    return extended.reshape(-1, detail.shape[1])


def shards(
    fine_coef,
    mid_leaf,
    mid_child,
    mid_parent,
    mid_refined,
    fine_nbr,
    mid_nbr,
    coarse_nbr,
    op_factor,
    term_weight,
):
    basis_order = op_factor.shape[-1]
    filters = two_scale(basis_order)
    mid_local = mid_child.shape[0]
    slots_dev = fine_coef.shape[0]
    coarse_count = coarse_nbr.shape[0]
    child_hot = (
        mid_child[:, :, None] == jnp.arange(slots_dev, dtype=jnp.int32)[None, None, :]
    ).astype(jnp.float32)
    refined = mid_refined.astype(jnp.float32)
    live_mask = jnp.einsum("mos,m->s", child_hot, refined, precision=exact_mode)
    children = fine_coef[mid_child].astype(jnp.float32)
    compressed = compress(children, filters)
    mid_source = jnp.where(
        mid_refined[:, None] > 0, compressed, mid_leaf.astype(jnp.float32)
    ).astype(jnp.bfloat16)
    mid_float = mid_source.astype(jnp.float32)
    spread = prolong(mid_float, filters)
    fine_from = jnp.einsum("mos,mok->sk", child_hot, spread, precision=exact_mode)
    fine_detail = (live_mask[:, None] * (fine_coef.astype(jnp.float32) - fine_from)).astype(
        jnp.bfloat16
    )
    parent = mid_parent // 8
    octant = mid_parent % 8
    octant_hot = (octant[:, None] == jnp.arange(8, dtype=jnp.int32)[None, :]).astype(jnp.float32)
    parent_hot = (parent[:, None] == jnp.arange(coarse_count, dtype=jnp.int32)[None, :]).astype(
        jnp.float32
    )
    placed = octant_hot[:, :, None] * mid_float[:, None, :]
    contribution = compress(placed, filters)
    partial_sum = jnp.dot(parent_hot.T, contribution, precision=exact_mode)
    coarse_source = lax.psum(partial_sum, ("gx", "gy", "gz"))
    fine_table = near_fine(fine_detail)
    fine_factor, fine_blocks = level_tables(op_factor[0], term_weight)
    fine_direct = apply_picked(
        fine_table, local_rows(fine_nbr, slots_dev), fine_factor, fine_blocks
    )
    parent_source = jnp.dot(parent_hot, coarse_source, precision=exact_mode)
    from_coarse = jnp.einsum(
        "mo,mok->mk", octant_hot, prolong(parent_source, filters), precision=exact_mode
    )
    mid_detail = (mid_float - from_coarse).astype(jnp.bfloat16)
    mid_table = near_mid(mid_detail)
    mid_factor, mid_blocks = level_tables(op_factor[1], term_weight)
    mid_direct = apply_picked(mid_table, local_rows(mid_nbr, mid_local), mid_factor, mid_blocks)
    coarse_table = coarse_source.astype(jnp.bfloat16)
    coarse_factor, coarse_blocks = level_tables(op_factor[2], term_weight)
    parent_out = apply_picked(coarse_table, coarse_nbr[parent], coarse_factor, coarse_blocks)
    mid_out = mid_direct + jnp.einsum(
        "mo,mok->mk", octant_hot, prolong(parent_out, filters), precision=exact_mode
    )
    fine_back = jnp.einsum(
        "mos,mok->sk", child_hot, prolong(mid_out, filters), precision=exact_mode
    )
    fine_out = live_mask[:, None] * (fine_direct + fine_back)
    return (fine_out, mid_out)


def solution(mesh):
    return jax.shard_map(
        shards,
        mesh=mesh,
        in_specs=(
            P(("gx", "gy", "gz"), None),
            P(("gx", "gy", "gz"), None),
            P(("gx", "gy", "gz"), None),
            P(("gx", "gy", "gz")),
            P(("gx", "gy", "gz")),
            P(("gx", "gy", "gz"), None),
            P(("gx", "gy", "gz"), None),
            P(),
            P(),
            P(),
        ),
        out_specs=(P(("gx", "gy", "gz"), None), P(("gx", "gy", "gz"), None)),
        check_vma=False,
    )
```

profile of v0, /device:TPU:10, one launch (start us, length us, event | category | flops | bytes accessed | tf_op | source)
XLA Modules:
  0.0 179.6 jit_solution(12119286320038687831)
XLA Ops:
  2.7 1.3 gather_fusion
  4.2 1.0 convolution_bitcast_fusion.38
  5.2 1.0 convolution_bitcast_fusion.44
  8.0 1.0 convolution_bitcast_fusion.37
  9.0 1.0 convolution_bitcast_fusion.43
  11.1 41.2 %psum.7 = f32[4,512]{1,0:T(4,128)S(1)} all-reduce(f32[4,512]{1,0:T(4,128)S(1)} %broadcast_multiply_fusion), channel_id=1, replica_groups=mesh['gx'=4,'gy'=4,'gz'=2] {'gx','gy','gz'}, use_global_device_ids=true, to_apply=%region_1.2 | all-reduce | flops 2048 | bytes 16384 | tf_op jit(solution)/shard_map/psum | solution.py:226
  52.7 1.0 fusion.102
  53.7 1.0 convolution_bitcast_fusion.41
  54.7 2.6 %convolution_bitcast_fusion.17 = f32[1,2,2,2,8,8,8]{5,6,4,2,1,3,0:T(8,128)S(1)} fusion(f32[2,8,8,1,1,1]{2,1,5,4,3,0:T(8,128)} %constant.328, f32[2,2,8,8,8]{4,3,2,0,1:T(8,128)S(1)} %convolution_bitcast_fusion.41), kind=kOutput, calls=%fused_computation.48 | convolution fusion | flops 393216 | bytes 25088 | tf_op jit(solution)/shard_map/bijxyr,lrz->bijlxyz/dot_general | solution.py:89
  57.7 1.9 %collective-permute-start.6 = (bf16[1,1,1,1,512]{4,2,1,0,3:T(2,128)(2,1)S(1)}, bf16[1,1,1,1,512]{4,2,1,0,3:T(2,128)(2,1)S(1)}, u32[]{:S(2)}, u32[]{:S(2)}) collective-permute-start(bf16[1,1,1,1,512]{4,2,1,0,3:T(2,128)(2,1)S(1)} %fusion.60), channel_id=1, source_target_pairs={{0,8},{8,16},{16,24},{1,9},{9,17},{17,25},{2,10},{10,18},{18,26},{... | collective-permute-start | bytes 3080 | tf_op jit(solution)/shard_map/ppermute | solution.py:19
  59.6 3.6 %collective-permute-start.7 = (bf16[1,1,1,1,512]{4,2,1,0,3:T(2,128)(2,1)S(1)}, bf16[1,1,1,1,512]{4,2,1,0,3:T(2,128)(2,1)S(1)}, u32[]{:S(2)}, u32[]{:S(2)}) collective-permute-start(bf16[1,1,1,1,512]{4,2,1,0,3:T(2,128)(2,1)S(1)} %fusion.60), channel_id=1, source_target_pairs={{8,0},{16,8},{24,16},{9,1},{17,9},{25,17},{10,2},{18,10},{26,18},{... | collective-permute-start | bytes 3080 | tf_op jit(solution)/shard_map/ppermute | solution.py:21
  64.1 1.9 %convolution_bitcast_fusion.18 = f32[1,2,2,2,8,8,8]{5,6,4,2,1,3,0:T(8,128)S(1)} fusion(f32[2,8,8,1,1,1]{2,1,5,4,3,0:T(8,128)S(1)} %copy-done.6, f32[2,2,8,8,8]{4,3,2,0,1:T(8,128)S(1)} %convolution_bitcast_fusion.42), kind=kOutput, calls=%fused_computation.49 | convolution fusion | flops 393216 | bytes 25088 | tf_op jit(solution)/shard_map/bijxyr,lrz->bijlxyz/dot_general | solution.py:89
  66.5 1.9 %collective-permute-start = (bf16[1,1,1,8,512]{4,3,2,1,0:T(8,128)(2,1)S(1)}, bf16[1,1,1,8,512]{4,3,2,1,0:T(8,128)(2,1)S(1)}, u32[]{:S(2)}, u32[]{:S(2)}) collective-permute-start(bf16[1,1,1,8,512]{4,3,2,1,0:T(8,128)(2,1)S(1)} %fusion.58), channel_id=1, source_target_pairs={{0,8},{8,16},{16,24},{1,9},{9,17},{17,25},{2,10},{10,18},{18,26},{... | collective-permute-start | bytes 24584 | tf_op jit(solution)/shard_map/ppermute | solution.py:19
  68.5 3.6 %collective-permute-start.1 = (bf16[1,1,1,8,512]{4,3,2,1,0:T(8,128)(2,1)S(1)}, bf16[1,1,1,8,512]{4,3,2,1,0:T(8,128)(2,1)S(1)}, u32[]{:S(2)}, u32[]{:S(2)}) collective-permute-start(bf16[1,1,1,8,512]{4,3,2,1,0:T(8,128)(2,1)S(1)} %fusion.58), channel_id=1, source_target_pairs={{8,0},{16,8},{24,16},{9,1},{17,9},{25,17},{10,2},{18,10},{26,18},{... | collective-permute-start | bytes 24584 | tf_op jit(solution)/shard_map/ppermute | solution.py:21
  75.8 1.5 convolution_bitcast_fusion.1
  77.2 1.3 convolution_bitcast_fusion
  78.9 1.3 convolution_bitcast_fusion.3
  80.2 1.3 convolution_bitcast_fusion.2
  81.9 1.3 convolution_bitcast_fusion.5
  83.2 1.3 convolution_bitcast_fusion.4
  84.8 1.0 fusion
  91.4 1.9 %convolution_bitcast_fusion.16 = f32[1,2,2,2,8,8,8]{5,6,4,2,1,3,0:T(8,128)S(1)} fusion(f32[2,8,8,1,1,1]{2,1,5,4,3,0:T(8,128)S(1)} %copy-done.6, f32[2,2,8,8,8]{4,3,2,0,1:T(8,128)S(1)} %convolution_bitcast_fusion.40), kind=kOutput, calls=%fused_computation.47 | convolution fusion | flops 393216 | bytes 25088 | tf_op jit(solution)/shard_map/bijxyr,lrz->bijlxyz/dot_general | solution.py:89
  97.1 2.0 %multiply_convert_fusion.1 = bf16[3,3,2048,64]{2,3,1,0:T(8,128)(2,1)} fusion(f32[3,2048,64]{1,2,0:T(8,128)S(1)} %fusion.155, f32[3,2048,64]{1,2,0:T(8,128)S(1)} %convolution_multiply_fusion.1), kind=kLoop, calls=%fused_computation.5 | loop fusion | flops 2359296 | bytes 5505024 | tf_op jit(solution)/shard_map/convert_element_type | solution.py:120
  99.7 3.3 %collective-permute-start.8 = (bf16[3,1,1,1,512]{4,2,1,0,3:T(2,128)(2,1)S(1)}, bf16[3,1,1,1,512]{4,2,1,0,3:T(2,128)(2,1)S(1)}, u32[]{:S(2)}, u32[]{:S(2)}) collective-permute-start(bf16[3,1,1,1,512]{4,2,1,0,3:T(2,128)(2,1)S(1)} %pad_maximum_fusion.5), channel_id=1, source_target_pairs={{0,2},{2,4},{4,6},{1,3},{3,5},{5,7},{8,10},{10,12},{12,14},{9,11},... | collective-permute-start | bytes 9224 | tf_op jit(solution)/shard_map/ppermute | solution.py:19
  103.0 2.5 %collective-permute-start.9 = (bf16[3,1,1,1,512]{4,2,1,0,3:T(2,128)(2,1)S(1)}, bf16[3,1,1,1,512]{4,2,1,0,3:T(2,128)(2,1)S(1)}, u32[]{:S(2)}, u32[]{:S(2)}) collective-permute-start(bf16[3,1,1,1,512]{4,2,1,0,3:T(2,128)(2,1)S(1)} %pad_maximum_fusion.5), channel_id=1, source_target_pairs={{2,0},{4,2},{6,4},{3,1},{5,3},{7,5},{10,8},{12,10},{14,12},{11,9},... | collective-permute-start | bytes 9224 | tf_op jit(solution)/shard_map/ppermute | solution.py:21
  106.1 2.5 %collective-permute-done.9 = bf16[3,1,1,1,512]{4,2,1,0,3:T(2,128)(2,1)S(1)} collective-permute-done((bf16[3,1,1,1,512]{4,2,1,0,3:T(2,128)(2,1)S(1)}, bf16[3,1,1,1,512]{4,2,1,0,3:T(2,128)(2,1)S(1)}, u32[]{:S(2)}, u32[]{:S(2)}) %collective-permute-start.9) | collective-permute-done | bytes 3104 | tf_op jit(solution)/shard_map/ppermute | solution.py:21
  108.6 2.5 %collective-permute-start.10 = (bf16[3,3,1,1,512]{4,2,1,0,3:T(2,128)(2,1)S(1)}, bf16[3,3,1,1,512]{4,2,1,0,3:T(2,128)(2,1)S(1)}, u32[]{:S(2)}, u32[]{:S(2)}) collective-permute-start(bf16[3,3,1,1,512]{4,2,1,0,3:T(2,128)(2,1)S(1)} %pad_maximum_fusion.4), channel_id=1, source_target_pairs={{0,1},{2,3},{4,5},{6,7},{8,9},{10,11},{12,13},{14,15},{16,17},{18,... | collective-permute-start | bytes 27656 | tf_op jit(solution)/shard_map/ppermute | solution.py:19
  111.1 1.3 collective-permute-start.11
  112.4 2.3 %collective-permute-start.2 = (bf16[3,1,1,8,512]{4,3,2,1,0:T(8,128)(2,1)S(1)}, bf16[3,1,1,8,512]{4,3,2,1,0:T(8,128)(2,1)S(1)}, u32[]{:S(2)}, u32[]{:S(2)}) collective-permute-start(bf16[3,1,1,8,512]{4,3,2,1,0:T(8,128)(2,1)S(1)} %pad_maximum_fusion.3), channel_id=1, source_target_pairs={{0,2},{2,4},{4,6},{1,3},{3,5},{5,7},{8,10},{10,12},{12,14},{9,11},... | collective-permute-start | bytes 73736 | tf_op jit(solution)/shard_map/ppermute | solution.py:19
  114.7 3.7 %collective-permute-start.3 = (bf16[3,1,1,8,512]{4,3,2,1,0:T(8,128)(2,1)S(1)}, bf16[3,1,1,8,512]{4,3,2,1,0:T(8,128)(2,1)S(1)}, u32[]{:S(2)}, u32[]{:S(2)}) collective-permute-start(bf16[3,1,1,8,512]{4,3,2,1,0:T(8,128)(2,1)S(1)} %pad_maximum_fusion.3), channel_id=1, source_target_pairs={{2,0},{4,2},{6,4},{3,1},{5,3},{7,5},{10,8},{12,10},{14,12},{11,9},... | collective-permute-start | bytes 73736 | tf_op jit(solution)/shard_map/ppermute | solution.py:21
  122.6 1.1 fusion.69
  123.7 1.1 convolution_add_fusion.24
  124.8 1.1 convolution_add_fusion.23
  125.9 1.1 convolution_add_fusion.22
  127.1 1.1 convolution_add_fusion.21
  128.2 1.1 convolution_add_fusion.20
  129.4 1.1 convolution_add_fusion.19
  130.5 1.1 convolution_add_fusion.18
  131.6 1.1 convolution_add_fusion.17
  133.6 4.5 %collective-permute-start.4 = (bf16[3,3,1,8,512]{4,3,2,1,0:T(8,128)(2,1)S(1)}, bf16[3,3,1,8,512]{4,3,2,1,0:T(8,128)(2,1)S(1)}, u32[]{:S(2)}, u32[]{:S(2)}) collective-permute-start(bf16[3,3,1,8,512]{4,3,2,1,0:T(8,128)(2,1)S(1)} %pad_maximum_fusion.1), channel_id=1, source_target_pairs={{0,1},{2,3},{4,5},{6,7},{8,9},{10,11},{12,13},{14,15},{16,17},{18,... | collective-permute-start | bytes 221192 | tf_op jit(solution)/shard_map/ppermute | solution.py:19
  138.1 1.3 collective-permute-start.5
  139.4 1.9 %convolution_bitcast_fusion.15 = f32[1,2,2,2,8,8,8]{5,6,4,2,1,3,0:T(8,128)S(1)} fusion(f32[2,8,8,1,1,1]{2,1,5,4,3,0:T(8,128)S(1)} %copy-done.6, f32[2,2,8,8,8]{4,3,2,0,1:T(8,128)S(1)} %convolution_bitcast_fusion.39), kind=kOutput, calls=%fused_computation.46 | convolution fusion | flops 393216 | bytes 25088 | tf_op jit(solution)/shard_map/bijxyr,lrz->bijlxyz/dot_general | solution.py:89
  141.6 2.8 %collective-permute-done.5 = bf16[3,3,1,8,512]{4,3,2,1,0:T(8,128)(2,1)S(1)} collective-permute-done((bf16[3,3,1,8,512]{4,3,2,1,0:T(8,128)(2,1)S(1)}, bf16[3,3,1,8,512]{4,3,2,1,0:T(8,128)(2,1)S(1)}, u32[]{:S(2)}, u32[]{:S(2)}) %collective-permute-start.5) | collective-permute-done | bytes 73760 | tf_op jit(solution)/shard_map/ppermute | solution.py:21
  144.4 1.1 gather_fusion.1
  146.0 1.1 fusion.18
  147.2 1.1 fusion.17
  148.3 1.1 fusion.16
  149.4 1.1 fusion.15
  150.6 1.2 fusion.14
  151.7 1.1 fusion.13
  152.9 1.1 fusion.12
  154.7 2.2 %reshape.817 = bf16[64,2048]{1,0:T(8,128)(2,1)} reshape(bf16[8,8,32,64]{3,2,1,0:T(8,128)(2,1)} %fusion.18) | data formatting | bytes 524288 | tf_op jit(solution)/shard_map/while/body/eval_jaxpr/reshape | solution.py:135
  156.9 2.2 %reshape.820 = bf16[64,2048]{1,0:T(8,128)(2,1)} reshape(bf16[8,8,32,64]{3,2,1,0:T(8,128)(2,1)} %fusion.17) | data formatting | bytes 524288 | tf_op jit(solution)/shard_map/while/body/eval_jaxpr/reshape | solution.py:135
  159.1 2.2 %reshape.821 = bf16[64,2048]{1,0:T(8,128)(2,1)} reshape(bf16[8,8,32,64]{3,2,1,0:T(8,128)(2,1)} %fusion.16) | data formatting | bytes 524288 | tf_op jit(solution)/shard_map/while/body/eval_jaxpr/reshape | solution.py:135
  161.3 2.2 %reshape.822 = bf16[64,2048]{1,0:T(8,128)(2,1)} reshape(bf16[8,8,32,64]{3,2,1,0:T(8,128)(2,1)} %fusion.15) | data formatting | bytes 524288 | tf_op jit(solution)/shard_map/while/body/eval_jaxpr/reshape | solution.py:135
  163.5 2.2 %reshape.823 = bf16[64,2048]{1,0:T(8,128)(2,1)} reshape(bf16[8,8,32,64]{3,2,1,0:T(8,128)(2,1)} %fusion.14) | data formatting | bytes 524288 | tf_op jit(solution)/shard_map/while/body/eval_jaxpr/reshape | solution.py:135
  165.7 2.2 %reshape.824 = bf16[64,2048]{1,0:T(8,128)(2,1)} reshape(bf16[8,8,32,64]{3,2,1,0:T(8,128)(2,1)} %fusion.13) | data formatting | bytes 524288 | tf_op jit(solution)/shard_map/while/body/eval_jaxpr/reshape | solution.py:135
  168.0 2.2 %reshape.825 = bf16[64,2048]{1,0:T(8,128)(2,1)} reshape(bf16[8,8,32,64]{3,2,1,0:T(8,128)(2,1)} %fusion.12) | data formatting | bytes 524288 | tf_op jit(solution)/shard_map/while/body/eval_jaxpr/reshape | solution.py:135
  170.2 1.2 reshape.826
  171.8 1.2 fusion.70
  173.0 1.2 convolution_add_fusion.7
  174.2 1.2 convolution_add_fusion.6
  175.4 1.2 convolution_add_fusion.5
  176.5 1.2 convolution_add_fusion.4
  (187 shorter events, 29.5 us)
Async XLA Ops:
  0.6 62.9 %copy-start.5 = (f32[2,8,8,1]{2,1,3,0:T(8,128)S(1)}, f32[2,8,8,1]{2,1,3,0:T(8,128)}, u32[]{:S(2)}) copy-start(f32[2,8,8,1]{2,1,3,0:T(8,128)} %constant.330) | copy-start | bytes 1540
  0.6 63.1 %copy-start.7 = (f32[2,8,8,1,1]{2,1,4,3,0:T(8,128)S(1)}, f32[2,8,8,1,1]{2,1,4,3,0:T(8,128)}, u32[]{:S(2)}) copy-start(f32[2,8,8,1,1]{2,1,4,3,0:T(8,128)} %constant.329) | copy-start | bytes 1540
  0.7 63.4 %copy-start.6 = (f32[2,8,8,1,1,1]{2,1,5,4,3,0:T(8,128)S(1)}, f32[2,8,8,1,1,1]{2,1,5,4,3,0:T(8,128)}, u32[]{:S(2)}) copy-start(f32[2,8,8,1,1,1]{2,1,5,4,3,0:T(8,128)} %constant.328) | copy-start | bytes 1540
  0.7 62.6 %copy-start.13 = (s32[1,8]{1,0:T(1,128)S(1)}, s32[1,8]{1,0:T(1,128)}, u32[]{:S(2)}) copy-start(s32[1,8]{1,0:T(1,128)} %param.13) | copy-start | bytes 100
  4.0 62.3 %copy-start.4 = (bf16[8,512]{1,0:T(8,128)(2,1)S(1)}, bf16[8,512]{1,0:T(8,128)(2,1)}, u32[]{:S(2)}) copy-start(bf16[8,512]{1,0:T(8,128)(2,1)} %param.11) | copy-start | bytes 24580
  4.2 68.0 %copy-start.3 = (f32[3,32,3,8,8]{1,4,3,2,0:T(8,128)S(1)}, f32[3,32,3,8,8]{1,4,3,2,0:T(8,128)}, u32[]{:S(2)}) copy-start(f32[3,32,3,8,8]{1,4,3,2,0:T(8,128)} %param.19) | copy-start | bytes 221188
  9.0 63.3 %copy-start.12 = (s32[4,27]{1,0:T(4,128)S(1)}, s32[4,27]{1,0:T(4,128)}, u32[]{:S(2)}) copy-start(s32[4,27]{1,0:T(4,128)} %param.18) | copy-start | bytes 1300
  52.4 20.6 %copy-start.10 = (s32[1,27]{1,0:T(1,128)S(1)}, s32[1,27]{1,0:T(1,128)}, u32[]{:S(2)}) copy-start(s32[1,27]{1,0:T(1,128)} %param.17) | copy-start | bytes 328
  57.7 42.0 %collective-permute-start.6 = (bf16[1,1,1,1,512]{4,2,1,0,3:T(2,128)(2,1)S(1)}, bf16[1,1,1,1,512]{4,2,1,0,3:T(2,128)(2,1)S(1)}, u32[]{:S(2)}, u32[]{:S(2)}) collective-permute-start(bf16[1,1,1,1,512]{4,2,1,0,3:T(2,128)(2,1)S(1)} %fusion.60), channel_id=1, source_target_pairs={{0,8},{8,16},{16,24},{1,9},{9,17},{17,25},{2,10},{10,18},{18,26},{... | collective-permute-start | bytes 3080 | tf_op jit(solution)/shard_map/ppermute | solution.py:19
  59.6 40.1 %collective-permute-start.7 = (bf16[1,1,1,1,512]{4,2,1,0,3:T(2,128)(2,1)S(1)}, bf16[1,1,1,1,512]{4,2,1,0,3:T(2,128)(2,1)S(1)}, u32[]{:S(2)}, u32[]{:S(2)}) collective-permute-start(bf16[1,1,1,1,512]{4,2,1,0,3:T(2,128)(2,1)S(1)} %fusion.60), channel_id=1, source_target_pairs={{8,0},{16,8},{24,16},{9,1},{17,9},{25,17},{10,2},{18,10},{26,18},{... | collective-permute-start | bytes 3080 | tf_op jit(solution)/shard_map/ppermute | solution.py:21
  66.5 45.8 %collective-permute-start = (bf16[1,1,1,8,512]{4,3,2,1,0:T(8,128)(2,1)S(1)}, bf16[1,1,1,8,512]{4,3,2,1,0:T(8,128)(2,1)S(1)}, u32[]{:S(2)}, u32[]{:S(2)}) collective-permute-start(bf16[1,1,1,8,512]{4,3,2,1,0:T(8,128)(2,1)S(1)} %fusion.58), channel_id=1, source_target_pairs={{0,8},{8,16},{16,24},{1,9},{9,17},{17,25},{2,10},{10,18},{18,26},{... | collective-permute-start | bytes 24584 | tf_op jit(solution)/shard_map/ppermute | solution.py:19
  68.5 43.9 %collective-permute-start.1 = (bf16[1,1,1,8,512]{4,3,2,1,0:T(8,128)(2,1)S(1)}, bf16[1,1,1,8,512]{4,3,2,1,0:T(8,128)(2,1)S(1)}, u32[]{:S(2)}, u32[]{:S(2)}) collective-permute-start(bf16[1,1,1,8,512]{4,3,2,1,0:T(8,128)(2,1)S(1)} %fusion.58), channel_id=1, source_target_pairs={{8,0},{16,8},{24,16},{9,1},{17,9},{25,17},{10,2},{18,10},{26,18},{... | collective-permute-start | bytes 24584 | tf_op jit(solution)/shard_map/ppermute | solution.py:21
  77.2 7.4 %copy-start.11 = (f32[32]{0:T(128)S(1)}, f32[32]{0:T(128)}, u32[]{:S(2)}) copy-start(f32[32]{0:T(128)} %param.20) | copy-start | bytes 388
  91.4 4.0 %copy-start.9 = (s32[8,27]{1,0:T(8,128)S(1)}, s32[8,27]{1,0:T(8,128)}, u32[]{:S(2)}) copy-start(s32[8,27]{1,0:T(8,128)} %param.16) | copy-start | bytes 2596
  99.7 6.3 %collective-permute-start.8 = (bf16[3,1,1,1,512]{4,2,1,0,3:T(2,128)(2,1)S(1)}, bf16[3,1,1,1,512]{4,2,1,0,3:T(2,128)(2,1)S(1)}, u32[]{:S(2)}, u32[]{:S(2)}) collective-permute-start(bf16[3,1,1,1,512]{4,2,1,0,3:T(2,128)(2,1)S(1)} %pad_maximum_fusion.5), channel_id=1, source_target_pairs={{0,2},{2,4},{4,6},{1,3},{3,5},{5,7},{8,10},{10,12},{12,14},{9,11},... | collective-permute-start | bytes 9224 | tf_op jit(solution)/shard_map/ppermute | solution.py:19
  103.0 5.5 %collective-permute-start.9 = (bf16[3,1,1,1,512]{4,2,1,0,3:T(2,128)(2,1)S(1)}, bf16[3,1,1,1,512]{4,2,1,0,3:T(2,128)(2,1)S(1)}, u32[]{:S(2)}, u32[]{:S(2)}) collective-permute-start(bf16[3,1,1,1,512]{4,2,1,0,3:T(2,128)(2,1)S(1)} %pad_maximum_fusion.5), channel_id=1, source_target_pairs={{2,0},{4,2},{6,4},{3,1},{5,3},{7,5},{10,8},{12,10},{14,12},{11,9},... | collective-permute-start | bytes 9224 | tf_op jit(solution)/shard_map/ppermute | solution.py:21
  108.6 9.9 %collective-permute-start.10 = (bf16[3,3,1,1,512]{4,2,1,0,3:T(2,128)(2,1)S(1)}, bf16[3,3,1,1,512]{4,2,1,0,3:T(2,128)(2,1)S(1)}, u32[]{:S(2)}, u32[]{:S(2)}) collective-permute-start(bf16[3,3,1,1,512]{4,2,1,0,3:T(2,128)(2,1)S(1)} %pad_maximum_fusion.4), channel_id=1, source_target_pairs={{0,1},{2,3},{4,5},{6,7},{8,9},{10,11},{12,13},{14,15},{16,17},{18,... | collective-permute-start | bytes 27656 | tf_op jit(solution)/shard_map/ppermute | solution.py:19
  111.1 7.4 %collective-permute-start.11 = (bf16[3,3,1,1,512]{4,2,1,0,3:T(2,128)(2,1)S(1)}, bf16[3,3,1,1,512]{4,2,1,0,3:T(2,128)(2,1)S(1)}, u32[]{:S(2)}, u32[]{:S(2)}) collective-permute-start(bf16[3,3,1,1,512]{4,2,1,0,3:T(2,128)(2,1)S(1)} %pad_maximum_fusion.4), channel_id=1, source_target_pairs={{1,0},{3,2},{5,4},{7,6},{9,8},{11,10},{13,12},{15,14},{17,16},{19,... | collective-permute-start | bytes 27656 | tf_op jit(solution)/shard_map/ppermute | solution.py:21
  112.4 21.1 %collective-permute-start.2 = (bf16[3,1,1,8,512]{4,3,2,1,0:T(8,128)(2,1)S(1)}, bf16[3,1,1,8,512]{4,3,2,1,0:T(8,128)(2,1)S(1)}, u32[]{:S(2)}, u32[]{:S(2)}) collective-permute-start(bf16[3,1,1,8,512]{4,3,2,1,0:T(8,128)(2,1)S(1)} %pad_maximum_fusion.3), channel_id=1, source_target_pairs={{0,2},{2,4},{4,6},{1,3},{3,5},{5,7},{8,10},{10,12},{12,14},{9,11},... | collective-permute-start | bytes 73736 | tf_op jit(solution)/shard_map/ppermute | solution.py:19
  114.7 18.8 %collective-permute-start.3 = (bf16[3,1,1,8,512]{4,3,2,1,0:T(8,128)(2,1)S(1)}, bf16[3,1,1,8,512]{4,3,2,1,0:T(8,128)(2,1)S(1)}, u32[]{:S(2)}, u32[]{:S(2)}) collective-permute-start(bf16[3,1,1,8,512]{4,3,2,1,0:T(8,128)(2,1)S(1)} %pad_maximum_fusion.3), channel_id=1, source_target_pairs={{2,0},{4,2},{6,4},{3,1},{5,3},{7,5},{10,8},{12,10},{14,12},{11,9},... | collective-permute-start | bytes 73736 | tf_op jit(solution)/shard_map/ppermute | solution.py:21
  132.8 12.9 %copy-start.8 = (f32[512]{0:T(512)}, f32[512]{0:T(512)S(1)}, u32[]{:S(2)}) copy-start(f32[512]{0:T(512)S(1)} %add.348) | copy-start | bytes 6148
  133.6 8.0 %collective-permute-start.4 = (bf16[3,3,1,8,512]{4,3,2,1,0:T(8,128)(2,1)S(1)}, bf16[3,3,1,8,512]{4,3,2,1,0:T(8,128)(2,1)S(1)}, u32[]{:S(2)}, u32[]{:S(2)}) collective-permute-start(bf16[3,3,1,8,512]{4,3,2,1,0:T(8,128)(2,1)S(1)} %pad_maximum_fusion.1), channel_id=1, source_target_pairs={{0,1},{2,3},{4,5},{6,7},{8,9},{10,11},{12,13},{14,15},{16,17},{18,... | collective-permute-start | bytes 221192 | tf_op jit(solution)/shard_map/ppermute | solution.py:19
  138.1 6.2 %collective-permute-start.5 = (bf16[3,3,1,8,512]{4,3,2,1,0:T(8,128)(2,1)S(1)}, bf16[3,3,1,8,512]{4,3,2,1,0:T(8,128)(2,1)S(1)}, u32[]{:S(2)}, u32[]{:S(2)}) collective-permute-start(bf16[3,3,1,8,512]{4,3,2,1,0:T(8,128)(2,1)S(1)} %pad_maximum_fusion.1), channel_id=1, source_target_pairs={{1,0},{3,2},{5,4},{7,6},{9,8},{11,10},{13,12},{15,14},{17,16},{19,... | collective-permute-start | bytes 221192 | tf_op jit(solution)/shard_map/ppermute | solution.py:21
  171.3 6.8 %copy-start = (bf16[64,2048]{1,0:T(8,128)(2,1)S(1)}, bf16[64,2048]{1,0:T(8,128)(2,1)}, u32[]{:S(2)}) copy-start(bf16[64,2048]{1,0:T(8,128)(2,1)} %reshape.826) | copy-start | bytes 786436
  171.8 5.9 %copy-start.2 = (bf16[64,2048]{1,0:T(8,128)(2,1)S(1)}, bf16[64,2048]{1,0:T(8,128)(2,1)}, u32[]{:S(2)}) copy-start(bf16[64,2048]{1,0:T(8,128)(2,1)} %reshape.824) | copy-start | bytes 786436
  171.8 6.2 %copy-start.1 = (bf16[64,2048]{1,0:T(8,128)(2,1)S(1)}, bf16[64,2048]{1,0:T(8,128)(2,1)}, u32[]{:S(2)}) copy-start(bf16[64,2048]{1,0:T(8,128)(2,1)} %reshape.825) | copy-start | bytes 786436
where the time goes:
time: 181 us; the launch traced here: 180 us
  matrix products  64.1 us (35%)
  blocking collectives  41.2 us (23%)
  starting transfers between devices  32.6 us (18%)
  local copies, waits for them, and re-layouts  28 us (15%)
  other arithmetic  5.35 us (3%)
  waiting for transfers between devices  5.27 us (3%)
  between operations  3.01 us (2%)
    psum x1, blocking collectives, shards(): coarse_source = lax.psum(partial_sum, ('gx', 'gy', 'gz'))  41.2 us
    reshape x27, local copies, waits for them, and re-layouts, apply_boxes(): flat_terms = mixed_terms.reshape(box_count * basis_order, -1)  19.5 us
    dot_general x27, matrix products, apply_boxes(): jnp.dot(flat_terms, blocks[along_y, along_z], preferred_element_type=jnp....  18.6 us
    ppermute x6, starting transfers between devices, padded_2(): lax.ppermute(tail, axis, [(i, (i + 1) % count) for i in range(ends)])  16.5 us
    ppermute x6, starting transfers between devices, padded_2(): lax.ppermute(head, axis, [((i + 1) % count, i) for i in range(ends)])  16.1 us
    dot_general x27, matrix products, apply_boxes(): jnp.einsum('mdax,bdxq->bamq', factor_bf, picked, preferred_element_type=j...  12.5 us
    dot_general x4, matrix products, prolong(): jnp.einsum('bijxyr,lrz->bijlxyz', section_two, filters, precision=exact_m...  8.2 us
    unnamed x6, matrix products  7.83 us
  transfers between devices with their start and end apart: 12, of which 2 were waited for; matrix products, arithmetic and copies ran while one was open for 27% of the time, Pallas kernels for 0%

commit v1 on v0

--- a/solution.py
+++ b/solution.py
@@ -223,7 +223,7 @@
     placed = octant_hot[:, :, None] * mid_float[:, None, :]
     contribution = compress(placed, filters)
     partial_sum = jnp.dot(parent_hot.T, contribution, precision=exact_mode)
-    coarse_source = lax.psum(partial_sum, ("gx", "gy", "gz"))
+    coarse_source = jnp.sum(lax.all_gather(partial_sum, ("gx", "gy", "gz")), axis=0)
     fine_table = near_fine(fine_detail)
     fine_factor, fine_blocks = level_tables(op_factor[0], term_weight)
     fine_direct = apply_picked(

time: 181 us -> 202 us (1.12)
  blocking collectives: 41.2 us -> 66 us
  matrix products: 64.1 us -> 62 us
    all_gather x0 -> x1, blocking collectives: none -> 66 us  [shards(): lax.all_gather(partial_sum, ('gx', 'gy', 'gz'))]
    psum x1 -> x0, blocking collectives: 41.2 us -> none  [shards(): coarse_source = lax.psum(partial_sum, ('gx', 'gy', 'gz'))]
  transfers between devices with their start and end apart: 12 -> 12, of which waited for: 2 -> 2; matrix products, arithmetic and copies ran while one was open for 27% -> 24% of each run, Pallas kernels for 0% -> 0%
where the time goes in v1:
time: 202 us; the launch traced here: 200 us
  blocking collectives  66 us (33%)
  matrix products  62 us (31%)
  starting transfers between devices  32.1 us (16%)
  local copies, waits for them, and re-layouts  28 us (14%)
  other arithmetic  5.45 us (3%)
  waiting for transfers between devices  3.62 us (2%)
  between operations  3.01 us (1%)
    all_gather x1, blocking collectives, shards(): lax.all_gather(partial_sum, ('gx', 'gy', 'gz'))  66 us
    reshape x27, local copies, waits for them, and re-layouts, apply_boxes(): flat_terms = mixed_terms.reshape(box_count * basis_order, -1)  19.5 us
    dot_general x27, matrix products, apply_boxes(): jnp.dot(flat_terms, blocks[along_y, along_z], preferred_element_type=jnp....  18.6 us
    ppermute x6, starting transfers between devices, padded_2(): lax.ppermute(head, axis, [((i + 1) % count, i) for i in range(ends)])  17.1 us
    ppermute x6, starting transfers between devices, padded_2(): lax.ppermute(tail, axis, [(i, (i + 1) % count) for i in range(ends)])  15 us
    dot_general x27, matrix products, apply_boxes(): jnp.einsum('mdax,bdxq->bamq', factor_bf, picked, preferred_element_type=j...  12.5 us
    unnamed x6, matrix products  7.83 us
    dot_general x4, matrix products, prolong(): jnp.einsum('bijxyr,lrz->bijlxyz', section_two, filters, precision=exact_m...  7.5 us
  transfers between devices with their start and end apart: 12, of which 2 were waited for; matrix products, arithmetic and copies ran while one was open for 24% of the time, Pallas kernels for 0%

profile of v1, /device:TPU:10, one launch (start us, length us, event | category | flops | bytes accessed | tf_op | source)
XLA Modules:
  0.0 200.1 jit_solution(10864366185902436228)
XLA Ops:
  2.7 1.3 gather_fusion
  4.2 1.0 convolution_bitcast_fusion.38
  5.1 1.0 convolution_bitcast_fusion.44
  6.1 0.9 convolution_bitcast_fusion.46
  8.0 1.0 convolution_bitcast_fusion.37
  9.0 1.0 convolution_bitcast_fusion.43
  10.0 0.9 convolution_bitcast_fusion.45
  11.0 66.0 %all-gather.1 = f32[32,4,512]{2,1,0:T(4,128)S(1)} all-gather(f32[1,4,512]{2,1,0:T(4,128)S(1)} %multiply_bitcast_fusion), channel_id=2, replica_groups=mesh['gx'=4,'gy'=4,'gz'=2] {'gx','gy','gz'}, dimensions={0}, use_global_device_ids=true | all-gather | bytes 270336 | tf_op jit(solution)/shard_map/all_gather | solution.py:226
  78.2 1.9 convolution_bitcast_fusion.17
  80.5 1.9 collective-permute-start.6
  82.4 3.6 %collective-permute-start.7 = (bf16[1,1,1,1,512]{4,2,1,0,3:T(2,128)(2,1)S(1)}, bf16[1,1,1,1,512]{4,2,1,0,3:T(2,128)(2,1)S(1)}, u32[]{:S(2)}, u32[]{:S(2)}) collective-permute-start(bf16[1,1,1,1,512]{4,2,1,0,3:T(2,128)(2,1)S(1)} %fusion.60), channel_id=1, source_target_pairs={{8,0},{16,8},{24,16},{9,1},{17,9},{25,17},{10,2},{18,10},{26,18},{... | collective-permute-start | bytes 3080 | tf_op jit(solution)/shard_map/ppermute | solution.py:21
  86.8 1.9 convolution_bitcast_fusion.18
  89.3 1.9 collective-permute-start
  91.2 3.6 %collective-permute-start.1 = (bf16[1,1,1,8,512]{4,3,2,1,0:T(8,128)(2,1)S(1)}, bf16[1,1,1,8,512]{4,3,2,1,0:T(8,128)(2,1)S(1)}, u32[]{:S(2)}, u32[]{:S(2)}) collective-permute-start(bf16[1,1,1,8,512]{4,3,2,1,0:T(8,128)(2,1)S(1)} %fusion.58), channel_id=1, source_target_pairs={{8,0},{16,8},{24,16},{9,1},{17,9},{25,17},{10,2},{18,10},{26,18},{... | collective-permute-start | bytes 24584 | tf_op jit(solution)/shard_map/ppermute | solution.py:21
  98.5 1.5 convolution_bitcast_fusion.1
  100.0 1.3 convolution_bitcast_fusion
  101.7 1.3 convolution_bitcast_fusion.3
  102.9 1.3 convolution_bitcast_fusion.2
  104.6 1.3 convolution_bitcast_fusion.5
  105.9 1.3 convolution_bitcast_fusion.4
  107.5 1.0 fusion
  114.2 1.9 convolution_bitcast_fusion.16
  119.9 2.0 multiply_convert_fusion.1
  122.5 1.9 collective-permute-start.8
  124.4 4.6 %collective-permute-start.9 = (bf16[3,1,1,1,512]{4,2,1,0,3:T(2,128)(2,1)S(1)}, bf16[3,1,1,1,512]{4,2,1,0,3:T(2,128)(2,1)S(1)}, u32[]{:S(2)}, u32[]{:S(2)}) collective-permute-start(bf16[3,1,1,1,512]{4,2,1,0,3:T(2,128)(2,1)S(1)} %pad_maximum_fusion.5), channel_id=1, source_target_pairs={{2,0},{4,2},{6,4},{3,1},{5,3},{7,5},{10,8},{12,10},{14,12},{11,9},... | collective-permute-start | bytes 9224 | tf_op jit(solution)/shard_map/ppermute | solution.py:21
  130.3 1.3 collective-permute-start.10
  131.6 1.3 collective-permute-start.11
  133.0 3.4 %collective-permute-start.2 = (bf16[3,1,1,8,512]{4,3,2,1,0:T(8,128)(2,1)S(1)}, bf16[3,1,1,8,512]{4,3,2,1,0:T(8,128)(2,1)S(1)}, u32[]{:S(2)}, u32[]{:S(2)}) collective-permute-start(bf16[3,1,1,8,512]{4,3,2,1,0:T(8,128)(2,1)S(1)} %pad_maximum_fusion.3), channel_id=1, source_target_pairs={{0,2},{2,4},{4,6},{1,3},{3,5},{5,7},{8,10},{10,12},{12,14},{9,11},... | collective-permute-start | bytes 73736 | tf_op jit(solution)/shard_map/ppermute | solution.py:19
  136.4 2.7 %collective-permute-start.3 = (bf16[3,1,1,8,512]{4,3,2,1,0:T(8,128)(2,1)S(1)}, bf16[3,1,1,8,512]{4,3,2,1,0:T(8,128)(2,1)S(1)}, u32[]{:S(2)}, u32[]{:S(2)}) collective-permute-start(bf16[3,1,1,8,512]{4,3,2,1,0:T(8,128)(2,1)S(1)} %pad_maximum_fusion.3), channel_id=1, source_target_pairs={{2,0},{4,2},{6,4},{3,1},{5,3},{7,5},{10,8},{12,10},{14,12},{11,9},... | collective-permute-start | bytes 73736 | tf_op jit(solution)/shard_map/ppermute | solution.py:21
  143.1 1.1 fusion.69
  144.3 1.1 convolution_add_fusion.24
  145.4 1.1 convolution_add_fusion.23
  146.5 1.1 convolution_add_fusion.22
  147.7 1.1 convolution_add_fusion.21
  148.8 1.1 convolution_add_fusion.20
  149.9 1.1 convolution_add_fusion.19
  151.1 1.1 convolution_add_fusion.18
  152.2 1.1 convolution_add_fusion.17
  154.2 4.5 %collective-permute-start.4 = (bf16[3,3,1,8,512]{4,3,2,1,0:T(8,128)(2,1)S(1)}, bf16[3,3,1,8,512]{4,3,2,1,0:T(8,128)(2,1)S(1)}, u32[]{:S(2)}, u32[]{:S(2)}) collective-permute-start(bf16[3,3,1,8,512]{4,3,2,1,0:T(8,128)(2,1)S(1)} %pad_maximum_fusion.1), channel_id=1, source_target_pairs={{0,1},{2,3},{4,5},{6,7},{8,9},{10,11},{12,13},{14,15},{16,17},{18,... | collective-permute-start | bytes 221192 | tf_op jit(solution)/shard_map/ppermute | solution.py:19
  158.7 1.3 collective-permute-start.5
  160.0 1.9 convolution_bitcast_fusion.15
  162.2 2.8 %collective-permute-done.5 = bf16[3,3,1,8,512]{4,3,2,1,0:T(8,128)(2,1)S(1)} collective-permute-done((bf16[3,3,1,8,512]{4,3,2,1,0:T(8,128)(2,1)S(1)}, bf16[3,3,1,8,512]{4,3,2,1,0:T(8,128)(2,1)S(1)}, u32[]{:S(2)}, u32[]{:S(2)}) %collective-permute-start.5) | collective-permute-done | bytes 73760 | tf_op jit(solution)/shard_map/ppermute | solution.py:21
  165.0 1.1 gather_fusion.1
  166.6 1.1 fusion.18
  167.8 1.1 fusion.17
  168.9 1.1 fusion.16
  170.0 1.1 fusion.15
  171.2 1.2 fusion.14
  172.3 1.1 fusion.13
  173.5 1.1 fusion.12
  175.3 2.2 %reshape.817 = bf16[64,2048]{1,0:T(8,128)(2,1)} reshape(bf16[8,8,32,64]{3,2,1,0:T(8,128)(2,1)} %fusion.18) | data formatting | bytes 524288 | tf_op jit(solution)/shard_map/while/body/eval_jaxpr/reshape | solution.py:135
  177.5 2.2 %reshape.820 = bf16[64,2048]{1,0:T(8,128)(2,1)} reshape(bf16[8,8,32,64]{3,2,1,0:T(8,128)(2,1)} %fusion.17) | data formatting | bytes 524288 | tf_op jit(solution)/shard_map/while/body/eval_jaxpr/reshape | solution.py:135
  179.7 2.2 %reshape.821 = bf16[64,2048]{1,0:T(8,128)(2,1)} reshape(bf16[8,8,32,64]{3,2,1,0:T(8,128)(2,1)} %fusion.16) | data formatting | bytes 524288 | tf_op jit(solution)/shard_map/while/body/eval_jaxpr/reshape | solution.py:135
  181.9 2.2 %reshape.822 = bf16[64,2048]{1,0:T(8,128)(2,1)} reshape(bf16[8,8,32,64]{3,2,1,0:T(8,128)(2,1)} %fusion.15) | data formatting | bytes 524288 | tf_op jit(solution)/shard_map/while/body/eval_jaxpr/reshape | solution.py:135
  184.1 2.2 %reshape.823 = bf16[64,2048]{1,0:T(8,128)(2,1)} reshape(bf16[8,8,32,64]{3,2,1,0:T(8,128)(2,1)} %fusion.14) | data formatting | bytes 524288 | tf_op jit(solution)/shard_map/while/body/eval_jaxpr/reshape | solution.py:135
  186.3 2.2 %reshape.824 = bf16[64,2048]{1,0:T(8,128)(2,1)} reshape(bf16[8,8,32,64]{3,2,1,0:T(8,128)(2,1)} %fusion.13) | data formatting | bytes 524288 | tf_op jit(solution)/shard_map/while/body/eval_jaxpr/reshape | solution.py:135
  188.5 2.2 %reshape.825 = bf16[64,2048]{1,0:T(8,128)(2,1)} reshape(bf16[8,8,32,64]{3,2,1,0:T(8,128)(2,1)} %fusion.12) | data formatting | bytes 524288 | tf_op jit(solution)/shard_map/while/body/eval_jaxpr/reshape | solution.py:135
  190.7 1.2 reshape.826
  192.4 1.2 fusion.70
  193.6 1.2 convolution_add_fusion.7
  194.8 1.2 convolution_add_fusion.6
  195.9 1.2 convolution_add_fusion.5
  197.1 1.2 convolution_add_fusion.4
  199.3 0.9 fusion.55
  (188 shorter events, 28.4 us)
Async XLA Ops:
  0.6 76.9 %copy-start.5 = (f32[2,8,8,1]{2,1,3,0:T(8,128)S(1)}, f32[2,8,8,1]{2,1,3,0:T(8,128)}, u32[]{:S(2)}) copy-start(f32[2,8,8,1]{2,1,3,0:T(8,128)} %constant.330) | copy-start | bytes 1540
  0.6 77.2 %copy-start.7 = (f32[2,8,8,1,1]{2,1,4,3,0:T(8,128)S(1)}, f32[2,8,8,1,1]{2,1,4,3,0:T(8,128)}, u32[]{:S(2)}) copy-start(f32[2,8,8,1,1]{2,1,4,3,0:T(8,128)} %constant.329) | copy-start | bytes 1540
  0.7 77.5 %copy-start.6 = (f32[2,8,8,1,1,1]{2,1,5,4,3,0:T(8,128)S(1)}, f32[2,8,8,1,1,1]{2,1,5,4,3,0:T(8,128)}, u32[]{:S(2)}) copy-start(f32[2,8,8,1,1,1]{2,1,5,4,3,0:T(8,128)} %constant.328) | copy-start | bytes 1540
  0.7 85.4 %copy-start.13 = (s32[1,8]{1,0:T(1,128)S(1)}, s32[1,8]{1,0:T(1,128)}, u32[]{:S(2)}) copy-start(s32[1,8]{1,0:T(1,128)} %param.13) | copy-start | bytes 100
  6.1 82.9 %copy-start.4 = (bf16[8,512]{1,0:T(8,128)(2,1)S(1)}, bf16[8,512]{1,0:T(8,128)(2,1)}, u32[]{:S(2)}) copy-start(bf16[8,512]{1,0:T(8,128)(2,1)} %param.11) | copy-start | bytes 24580
  7.1 87.8 %copy-start.3 = (f32[3,32,3,8,8]{1,4,3,2,0:T(8,128)S(1)}, f32[3,32,3,8,8]{1,4,3,2,0:T(8,128)}, u32[]{:S(2)}) copy-start(f32[3,32,3,8,8]{1,4,3,2,0:T(8,128)} %param.19) | copy-start | bytes 221188
  77.1 18.0 %copy-start.12 = (s32[4,27]{1,0:T(4,128)S(1)}, s32[4,27]{1,0:T(4,128)}, u32[]{:S(2)}) copy-start(s32[4,27]{1,0:T(4,128)} %param.18) | copy-start | bytes 1300
  77.2 18.5 %copy-start.10 = (s32[1,27]{1,0:T(1,128)S(1)}, s32[1,27]{1,0:T(1,128)}, u32[]{:S(2)}) copy-start(s32[1,27]{1,0:T(1,128)} %param.17) | copy-start | bytes 328
  80.5 42.0 %collective-permute-start.6 = (bf16[1,1,1,1,512]{4,2,1,0,3:T(2,128)(2,1)S(1)}, bf16[1,1,1,1,512]{4,2,1,0,3:T(2,128)(2,1)S(1)}, u32[]{:S(2)}, u32[]{:S(2)}) collective-permute-start(bf16[1,1,1,1,512]{4,2,1,0,3:T(2,128)(2,1)S(1)} %fusion.60), channel_id=1, source_target_pairs={{0,8},{8,16},{16,24},{1,9},{9,17},{17,25},{2,10},{10,18},{18,26},{... | collective-permute-start | bytes 3080 | tf_op jit(solution)/shard_map/ppermute | solution.py:19
  82.4 40.0 %collective-permute-start.7 = (bf16[1,1,1,1,512]{4,2,1,0,3:T(2,128)(2,1)S(1)}, bf16[1,1,1,1,512]{4,2,1,0,3:T(2,128)(2,1)S(1)}, u32[]{:S(2)}, u32[]{:S(2)}) collective-permute-start(bf16[1,1,1,1,512]{4,2,1,0,3:T(2,128)(2,1)S(1)} %fusion.60), channel_id=1, source_target_pairs={{8,0},{16,8},{24,16},{9,1},{17,9},{25,17},{10,2},{18,10},{26,18},{... | collective-permute-start | bytes 3080 | tf_op jit(solution)/shard_map/ppermute | solution.py:21
  89.3 43.7 %collective-permute-start = (bf16[1,1,1,8,512]{4,3,2,1,0:T(8,128)(2,1)S(1)}, bf16[1,1,1,8,512]{4,3,2,1,0:T(8,128)(2,1)S(1)}, u32[]{:S(2)}, u32[]{:S(2)}) collective-permute-start(bf16[1,1,1,8,512]{4,3,2,1,0:T(8,128)(2,1)S(1)} %fusion.58), channel_id=1, source_target_pairs={{0,8},{8,16},{16,24},{1,9},{9,17},{17,25},{2,10},{10,18},{18,26},{... | collective-permute-start | bytes 24584 | tf_op jit(solution)/shard_map/ppermute | solution.py:19
  91.2 41.8 %collective-permute-start.1 = (bf16[1,1,1,8,512]{4,3,2,1,0:T(8,128)(2,1)S(1)}, bf16[1,1,1,8,512]{4,3,2,1,0:T(8,128)(2,1)S(1)}, u32[]{:S(2)}, u32[]{:S(2)}) collective-permute-start(bf16[1,1,1,8,512]{4,3,2,1,0:T(8,128)(2,1)S(1)} %fusion.58), channel_id=1, source_target_pairs={{8,0},{16,8},{24,16},{9,1},{17,9},{25,17},{10,2},{18,10},{26,18},{... | collective-permute-start | bytes 24584 | tf_op jit(solution)/shard_map/ppermute | solution.py:21
  100.0 7.4 %copy-start.11 = (f32[32]{0:T(128)S(1)}, f32[32]{0:T(128)}, u32[]{:S(2)}) copy-start(f32[32]{0:T(128)} %param.20) | copy-start | bytes 388
  114.2 4.0 %copy-start.9 = (s32[8,27]{1,0:T(8,128)S(1)}, s32[8,27]{1,0:T(8,128)}, u32[]{:S(2)}) copy-start(s32[8,27]{1,0:T(8,128)} %param.16) | copy-start | bytes 2596
  122.5 7.0 %collective-permute-start.8 = (bf16[3,1,1,1,512]{4,2,1,0,3:T(2,128)(2,1)S(1)}, bf16[3,1,1,1,512]{4,2,1,0,3:T(2,128)(2,1)S(1)}, u32[]{:S(2)}, u32[]{:S(2)}) collective-permute-start(bf16[3,1,1,1,512]{4,2,1,0,3:T(2,128)(2,1)S(1)} %pad_maximum_fusion.5), channel_id=1, source_target_pairs={{0,2},{2,4},{4,6},{1,3},{3,5},{5,7},{8,10},{10,12},{12,14},{9,11},... | collective-permute-start | bytes 9224 | tf_op jit(solution)/shard_map/ppermute | solution.py:19
  124.4 5.9 %collective-permute-start.9 = (bf16[3,1,1,1,512]{4,2,1,0,3:T(2,128)(2,1)S(1)}, bf16[3,1,1,1,512]{4,2,1,0,3:T(2,128)(2,1)S(1)}, u32[]{:S(2)}, u32[]{:S(2)}) collective-permute-start(bf16[3,1,1,1,512]{4,2,1,0,3:T(2,128)(2,1)S(1)} %pad_maximum_fusion.5), channel_id=1, source_target_pairs={{2,0},{4,2},{6,4},{3,1},{5,3},{7,5},{10,8},{12,10},{14,12},{11,9},... | collective-permute-start | bytes 9224 | tf_op jit(solution)/shard_map/ppermute | solution.py:21
  130.3 8.7 %collective-permute-start.10 = (bf16[3,3,1,1,512]{4,2,1,0,3:T(2,128)(2,1)S(1)}, bf16[3,3,1,1,512]{4,2,1,0,3:T(2,128)(2,1)S(1)}, u32[]{:S(2)}, u32[]{:S(2)}) collective-permute-start(bf16[3,3,1,1,512]{4,2,1,0,3:T(2,128)(2,1)S(1)} %pad_maximum_fusion.4), channel_id=1, source_target_pairs={{0,1},{2,3},{4,5},{6,7},{8,9},{10,11},{12,13},{14,15},{16,17},{18,... | collective-permute-start | bytes 27656 | tf_op jit(solution)/shard_map/ppermute | solution.py:19
  131.6 7.4 %collective-permute-start.11 = (bf16[3,3,1,1,512]{4,2,1,0,3:T(2,128)(2,1)S(1)}, bf16[3,3,1,1,512]{4,2,1,0,3:T(2,128)(2,1)S(1)}, u32[]{:S(2)}, u32[]{:S(2)}) collective-permute-start(bf16[3,3,1,1,512]{4,2,1,0,3:T(2,128)(2,1)S(1)} %pad_maximum_fusion.4), channel_id=1, source_target_pairs={{1,0},{3,2},{5,4},{7,6},{9,8},{11,10},{13,12},{15,14},{17,16},{19,... | collective-permute-start | bytes 27656 | tf_op jit(solution)/shard_map/ppermute | solution.py:21
  133.0 21.1 %collective-permute-start.2 = (bf16[3,1,1,8,512]{4,3,2,1,0:T(8,128)(2,1)S(1)}, bf16[3,1,1,8,512]{4,3,2,1,0:T(8,128)(2,1)S(1)}, u32[]{:S(2)}, u32[]{:S(2)}) collective-permute-start(bf16[3,1,1,8,512]{4,3,2,1,0:T(8,128)(2,1)S(1)} %pad_maximum_fusion.3), channel_id=1, source_target_pairs={{0,2},{2,4},{4,6},{1,3},{3,5},{5,7},{8,10},{10,12},{12,14},{9,11},... | collective-permute-start | bytes 73736 | tf_op jit(solution)/shard_map/ppermute | solution.py:19
  136.4 17.8 %collective-permute-start.3 = (bf16[3,1,1,8,512]{4,3,2,1,0:T(8,128)(2,1)S(1)}, bf16[3,1,1,8,512]{4,3,2,1,0:T(8,128)(2,1)S(1)}, u32[]{:S(2)}, u32[]{:S(2)}) collective-permute-start(bf16[3,1,1,8,512]{4,3,2,1,0:T(8,128)(2,1)S(1)} %pad_maximum_fusion.3), channel_id=1, source_target_pairs={{2,0},{4,2},{6,4},{3,1},{5,3},{7,5},{10,8},{12,10},{14,12},{11,9},... | collective-permute-start | bytes 73736 | tf_op jit(solution)/shard_map/ppermute | solution.py:21
  153.4 12.9 %copy-start.8 = (f32[512]{0:T(512)}, f32[512]{0:T(512)S(1)}, u32[]{:S(2)}) copy-start(f32[512]{0:T(512)S(1)} %add.346) | copy-start | bytes 6148
  154.2 8.0 %collective-permute-start.4 = (bf16[3,3,1,8,512]{4,3,2,1,0:T(8,128)(2,1)S(1)}, bf16[3,3,1,8,512]{4,3,2,1,0:T(8,128)(2,1)S(1)}, u32[]{:S(2)}, u32[]{:S(2)}) collective-permute-start(bf16[3,3,1,8,512]{4,3,2,1,0:T(8,128)(2,1)S(1)} %pad_maximum_fusion.1), channel_id=1, source_target_pairs={{0,1},{2,3},{4,5},{6,7},{8,9},{10,11},{12,13},{14,15},{16,17},{18,... | collective-permute-start | bytes 221192 | tf_op jit(solution)/shard_map/ppermute | solution.py:19
  158.7 6.2 %collective-permute-start.5 = (bf16[3,3,1,8,512]{4,3,2,1,0:T(8,128)(2,1)S(1)}, bf16[3,3,1,8,512]{4,3,2,1,0:T(8,128)(2,1)S(1)}, u32[]{:S(2)}, u32[]{:S(2)}) collective-permute-start(bf16[3,3,1,8,512]{4,3,2,1,0:T(8,128)(2,1)S(1)} %pad_maximum_fusion.1), channel_id=1, source_target_pairs={{1,0},{3,2},{5,4},{7,6},{9,8},{11,10},{13,12},{15,14},{17,16},{19,... | collective-permute-start | bytes 221192 | tf_op jit(solution)/shard_map/ppermute | solution.py:21
  191.9 6.8 %copy-start = (bf16[64,2048]{1,0:T(8,128)(2,1)S(1)}, bf16[64,2048]{1,0:T(8,128)(2,1)}, u32[]{:S(2)}) copy-start(bf16[64,2048]{1,0:T(8,128)(2,1)} %reshape.826) | copy-start | bytes 786436
  192.4 5.9 %copy-start.2 = (bf16[64,2048]{1,0:T(8,128)(2,1)S(1)}, bf16[64,2048]{1,0:T(8,128)(2,1)}, u32[]{:S(2)}) copy-start(bf16[64,2048]{1,0:T(8,128)(2,1)} %reshape.824) | copy-start | bytes 786436
  192.4 6.2 %copy-start.1 = (bf16[64,2048]{1,0:T(8,128)(2,1)S(1)}, bf16[64,2048]{1,0:T(8,128)(2,1)}, u32[]{:S(2)}) copy-start(bf16[64,2048]{1,0:T(8,128)(2,1)} %reshape.825) | copy-start | bytes 786436
